TPU v7x, 32 devices: a whole 2x2x4 slice. The times are simulated.
32 devices in a mesh: dp: 2 (over x), context: 8 (over z, core), tensor: 2 (over y).
Axes of the slice: x: 2, y: 2, z: 4, core: 2. Of those that a mesh axis runs over, the one named last changes fastest.
Arguments:
- tokens: bfloat16 [4, 4096, 768], P('dp', 'context'), may hold values from -6 to 6
- documents: int32 [4, 4096], P('dp', 'context'), may hold values from 0 to 15, never falling along the last dimension, each value on 1 to 1024 neighbouring positions
- norm_gain: float32 [768], P(('dp', 'context')), may hold values from 0.5 to 1.5
- entry_weight: float32 [768, 2, 1536], P(('dp', 'context'), None, 'tensor'), may hold values from -0.21875 to 0.21875
- state_weight: float32 [768, 256], P(('dp', 'context')), may hold values from -0.21875 to 0.21875
- step_weight: float32 [768, 24], P(('dp', 'context'), 'tensor'), may hold values from -0.109375 to 0.109375
- inner_kernel: float32 [5, 1536], P(None, 'tensor'), may hold values from -0.5 to 0.5
- state_filter: float32 [5, 256], replicated, may hold values from -0.5 to 0.5
- step_bias: float32 [24], P('tensor'), may hold values from -7 to -3
- decay_log: float32 [24], P('tensor'), may hold values from -1 to 1.5
- skip_gain: float32 [24], P('tensor'), may hold values from 0.25 to 1
- gate_gain: float32 [1536], P('tensor'), may hold values from 0.5 to 1.5
- exit_weight: float32 [768, 1536], P(('dp', 'context'), 'tensor'), may hold values from -0.15625 to 0.15625
- cotangent: bfloat16 [4, 4096, 768], P('dp', 'context'), may hold values from -6 to 6
Outputs:
- block_out: bfloat16 [4, 4096, 768], P('dp', 'context')
- token_grad: float32 [4, 4096, 768], P('dp', 'context')
- norm_grad: float32 [768], P(('dp', 'context'))
- entry_grad: float32 [768, 2, 1536], P(('dp', 'context'), None, 'tensor')
- state_weight_gradient: float32 [768, 256], P(('dp', 'context'))
- step_weight_gradient: float32 [768, 24], P(('dp', 'context'), 'tensor')
- kernel_grad: float32 [5, 1536], P(None, 'tensor')
- filter_grad: float32 [5, 256], replicated
- bias_grad: float32 [24], P('tensor')
- decay_grad: float32 [24], P('tensor')
- skip_grad: float32 [24], P('tensor')
- gate_grad: float32 [1536], P('tensor')
- exit_weight_gradient: float32 [768, 1536], P(('dp', 'context'), 'tensor')
Inputs may be any that keep to these rules, and one draw needn't show every extreme that they name: `documents`: in each sequence the document numbers start at 0, never fall, every one of 0 to 15 occurs, each document has 1 to 1024 positions, and one has exactly 1024.
All inputs are finite; a program needn't handle non-finite values.
Results may differ from a plain program's by a relative error of at most 0.012.
The roundings to bfloat16 on the way count: a program that leaves them out, or rounds other values in their place, can miss the bound.
Values may be sent and summed in bfloat16 or wider, within the bound.
A program may use at most 256 MiB of HBM per device.

v0:
```python
import jax
import jax.numpy as jnp
from jax import lax
from jax.sharding import PartitionSpec as P

HEAD = 64
NSTATE = 128
CONV = 4
SPAN = 256
EPSILON = 1e-05
PRECISION_HIGH = lax.Precision.HIGHEST


def passed_along(x, axis, by):
    count = lax.axis_size(axis)
    pairs = [(i, i + by) for i in range(count) if 0 <= i + by < count]
    return lax.ppermute(x, axis, pairs)


def carried_in(value, axis, join, neutral, backward):
    count, mine = (lax.axis_size(axis), lax.axis_index(axis))
    pieces = jax.tree.map(lambda part: lax.all_gather(part, axis), value)
    if backward:
        pieces = jax.tree.map(lambda part: part[::-1], pieces)
        mine = count - 1 - mine
    so_far = jax.tree.map(
        lambda part, zero: jnp.full_like(part, 0) + jnp.asarray(zero, part.dtype), value, neutral
    )

    def hop(position, so_far):
        longer = join(so_far, jax.tree.map(lambda part: part[position], pieces))
        return jax.tree.map(lambda new, old: jnp.where(position < mine, new, old), longer, so_far)

    return lax.fori_loop(0, count - 1, hop, so_far)


def prepare(extended, step_unactivated, kernel, step_bias, decay_log, ids_before, documents):
    width = documents.shape[1]
    ids_extended = jnp.concatenate([ids_before, documents], axis=1)
    preact = kernel[CONV]
    for offset in range(CONV):
        match = (ids_extended[:, offset : offset + width] == documents).astype(jnp.float32)
        preact = preact + kernel[offset] * extended[:, offset : offset + width] * match[:, :, None]
    mixed = jax.nn.silu(preact)
    inner_width = mixed.shape[2] - 2 * NSTATE
    steps = jax.nn.softplus(step_unactivated + step_bias)
    return (
        mixed[:, :, :inner_width],
        mixed[:, :, inner_width : inner_width + NSTATE],
        mixed[:, :, inner_width + NSTATE :],
        -steps * jnp.exp(decay_log),
        steps,
    )


def span_summary(inner, writer, log_decay, steps, documents, before):
    seqs, width = documents.shape
    heads = steps.shape[2]
    cumulative = jnp.cumsum(log_decay, axis=1)
    final = cumulative[:, -1]
    tail = (
        (documents == documents[:, -1:]).astype(jnp.float32)[:, :, None]
        * jnp.exp(final[:, None, :] - cumulative)
        * steps
    )
    values = inner.reshape(seqs, width, heads, HEAD)
    local = jnp.einsum("suh,suhp,sun->shpn", tail, values, writer, precision=PRECISION_HIGH)
    keep = (documents[:, -1] == before).astype(jnp.float32)
    return (local, keep[:, None] * jnp.exp(final))


def span_output(inner, writer, reader, log_decay, steps, carry_in, documents, before):
    seqs, width = documents.shape
    heads = steps.shape[2]
    cumulative = jnp.cumsum(jnp.swapaxes(log_decay, 1, 2), axis=2)
    places = jnp.arange(width)
    same = (places[:, None] >= places[None, :])[None] & (
        documents[:, :, None] == documents[:, None, :]
    )
    spread = cumulative[:, :, :, None] - cumulative[:, :, None, :]
    decay = jnp.exp(jnp.where(same[:, None], spread, 0.0)) * same[:, None].astype(jnp.float32)
    scores = jnp.einsum("stn,sun->stu", reader, writer, precision=PRECISION_HIGH)
    weights = decay * scores[:, None] * jnp.swapaxes(steps, 1, 2)[:, :, None, :]
    values = inner.reshape(seqs, width, heads, HEAD)
    local = jnp.einsum("shtu,suhp->sthp", weights, values, precision=PRECISION_HIGH)
    opened = (documents == before[:, None]).astype(jnp.float32)
    carried = jnp.einsum("stn,shpn->sthp", reader, carry_in, precision=PRECISION_HIGH)
    growth = opened[:, :, None] * jnp.exp(jnp.swapaxes(cumulative, 1, 2))
    result = local + growth[:, :, :, None] * carried
    return result.reshape(seqs, width, heads * HEAD)


def span_bounds(documents, before):
    width = documents.shape[1]
    length = min(SPAN, width)
    bounds = []
    for index in range(width // length):
        first = index * length
        entry = before if index == 0 else documents[:, first - 1]
        bounds.append((first, first + length, entry))
    return bounds


def block_state(inner, writer, log_decay, steps, documents, before):
    state = None
    gain = None
    for first, last, entry in span_bounds(documents, before):
        local, factor = span_summary(
            inner[:, first:last],
            writer[:, first:last],
            log_decay[:, first:last],
            steps[:, first:last],
            documents[:, first:last],
            entry,
        )
        if state is None:
            state, gain = (local, factor)
        else:
            state = factor[:, :, None, None] * state + local
            gain = gain * factor
    return (state, gain)


def block_output(inner, writer, reader, log_decay, steps, carry_in, documents, before):
    pieces = []
    entering = carry_in
    for first, last, entry in span_bounds(documents, before):
        part_docs = documents[:, first:last]
        pieces.append(
            span_output(
                inner[:, first:last],
                writer[:, first:last],
                reader[:, first:last],
                log_decay[:, first:last],
                steps[:, first:last],
                entering,
                part_docs,
                entry,
            )
        )
        if last < documents.shape[1]:
            local, factor = span_summary(
                inner[:, first:last],
                writer[:, first:last],
                log_decay[:, first:last],
                steps[:, first:last],
                part_docs,
                entry,
            )
            entering = factor[:, :, None, None] * entering + local
    return jnp.concatenate(pieces, axis=1)


def combine(earlier, later):
    return (earlier[0] * later[0], later[0][:, :, None, None] * earlier[1] + later[1])


def body(
    tokens,
    documents,
    norm_gain,
    entry_weight,
    state_weight,
    step_weight,
    inner_kernel,
    state_filter,
    step_bias,
    decay_log,
    skip_gain,
    gate_gain,
    exit_weight,
    cotangent,
):
    position = lax.axis_index("context")
    inputs = tokens.astype(jnp.float32)
    masters = (
        norm_gain.astype(jnp.bfloat16),
        entry_weight.astype(jnp.bfloat16),
        state_weight.astype(jnp.bfloat16),
        step_weight.astype(jnp.bfloat16),
        exit_weight.astype(jnp.bfloat16),
    )
    gain_low, entry_reduced, state_low, step_reduced, exit_reduced = (
        lax.all_gather(masters[0], ("dp", "context"), axis=0, tiled=True),
        lax.all_gather(masters[1], ("dp", "context"), axis=0, tiled=True),
        lax.all_gather(masters[2], ("dp", "context"), axis=0, tiled=True),
        lax.all_gather(masters[3], ("dp", "context"), axis=0, tiled=True),
        lax.all_gather(masters[4], ("dp", "context"), axis=0, tiled=True),
    )
    scale = lax.rsqrt(jnp.mean(inputs * inputs, axis=-1, keepdims=True) + EPSILON)
    hidden_activation = (inputs * scale * gain_low.astype(jnp.float32)).astype(jnp.bfloat16)
    gate_preactivation = jnp.einsum(
        "bqm,mj->bqj", hidden_activation, entry_reduced[:, 0], preferred_element_type=jnp.float32
    )
    convolution_weight = jnp.concatenate([entry_reduced[:, 1], state_low], axis=1)
    convolution_input = jnp.einsum(
        "bqm,mj->bqj", hidden_activation, convolution_weight, preferred_element_type=jnp.float32
    ).astype(jnp.bfloat16)
    step_unactivated = jnp.einsum(
        "wje,en->wjn", hidden_activation, step_reduced, preferred_element_type=jnp.float32
    )
    edge_ids = passed_along(documents[:, -(CONV - 1) :], "context", 1)
    ids_before = jnp.where(position == 0, -1, edge_ids)
    before = ids_before[:, -1]
    edge_rows = passed_along(convolution_input[:, -(CONV - 1) :], "context", 1)
    extended = jnp.concatenate([edge_rows, convolution_input], axis=1).astype(jnp.float32)
    kernel = jnp.concatenate([inner_kernel, state_filter], axis=1)

    def prepare_local(extended, step_unactivated, kernel, step_bias, decay_log):
        return prepare(
            extended, step_unactivated, kernel, step_bias, decay_log, ids_before, documents
        )

    (inner, writer, reader, log_decay, steps), prepare_back = jax.vjp(
        prepare_local, extended, step_unactivated, kernel, step_bias, decay_log
    )

    def state_local(inner, writer, log_decay, steps):
        return block_state(inner, writer, log_decay, steps, documents, before)

    (state_here, carry_gain), state_back = jax.vjp(state_local, inner, writer, log_decay, steps)
    ones = jnp.ones_like(carry_gain)
    zeros = jnp.zeros_like(state_here)
    gain_in, carry_in = carried_in(
        (carry_gain, state_here), "context", combine, (ones, zeros), False
    )

    def output_local(inner, writer, reader, log_decay, steps, carry_in):
        return block_output(inner, writer, reader, log_decay, steps, carry_in, documents, before)

    scanned, output_back = jax.vjp(output_local, inner, writer, reader, log_decay, steps, carry_in)
    heads = steps.shape[2]
    skip_wide = jnp.repeat(skip_gain, HEAD)
    output = scanned + skip_wide * inner
    gate_act = jax.nn.silu(gate_preactivation)
    gated = output * gate_act
    square_sum = lax.psum(jnp.sum(gated * gated, axis=-1), "tensor")
    inner_total = gated.shape[-1] * lax.axis_size("tensor")
    normal = lax.rsqrt(square_sum / inner_total + EPSILON)[:, :, None]
    unit_activation = (gated * normal * gate_gain).astype(jnp.bfloat16)
    partial_value_sum = jnp.einsum(
        "yjr,pr->yjp", unit_activation, exit_reduced, preferred_element_type=jnp.float32
    )
    branch_path = lax.psum(partial_value_sum, "tensor")
    block_out = (inputs + branch_path).astype(jnp.bfloat16)
    gain_back, entry_backward, state_backward_weight, step_backward, exit_backward = (
        lax.all_gather(masters[0], ("dp", "context"), axis=0, tiled=True),
        lax.all_gather(masters[1], ("dp", "context"), axis=0, tiled=True),
        lax.all_gather(masters[2], ("dp", "context"), axis=0, tiled=True),
        lax.all_gather(masters[3], ("dp", "context"), axis=0, tiled=True),
        lax.all_gather(masters[4], ("dp", "context"), axis=0, tiled=True),
    )
    exit_weight_gradient = jnp.einsum(
        "yqr,yqj->rj", cotangent, unit_activation, preferred_element_type=jnp.float32
    )
    unit_activation_gradient = jnp.einsum(
        "bqm,mj->bqj", cotangent, exit_backward, preferred_element_type=jnp.float32
    )
    gate_grad = jnp.sum(unit_activation_gradient * gated * normal, axis=(0, 1))
    scaled = unit_activation_gradient * gate_gain
    cross = lax.psum(jnp.sum(scaled * gated, axis=-1), "tensor")[:, :, None]
    gated_grad = normal * scaled - normal * normal * normal * gated * cross / inner_total
    output_grad = gated_grad * gate_act
    sigma = jax.nn.sigmoid(gate_preactivation)
    gate_preactivation_gradient = (
        gated_grad * output * sigma * (1.0 + gate_preactivation * (1.0 - sigma))
    ).astype(jnp.bfloat16)
    seqs, width = documents.shape
    skip_grad = jnp.sum((output_grad * inner).reshape(seqs, width, heads, HEAD), axis=(0, 1, 3))
    inner_one, writer_one, reader_one, decay_one, steps_one, entering = output_back(output_grad)
    gain_out, adjoint = carried_in((carry_gain, entering), "context", combine, (ones, zeros), True)
    gain_cot = jnp.sum(adjoint * carry_in, axis=(2, 3))
    inner_two, writer_two, decay_two, steps_two = state_back((adjoint, gain_cot))
    writer_sum, reader_sum = lax.psum((writer_one + writer_two, reader_one), "tensor")
    extended_grad, step_raw_full, kernel_full, bias_grad, decay_grad = prepare_back(
        (
            inner_one + inner_two + skip_wide * output_grad,
            writer_sum,
            reader_sum,
            decay_one + decay_two,
            steps_one + steps_two,
        )
    )
    edge_grad = passed_along(extended_grad[:, : CONV - 1], "context", -1)
    conv_part = extended_grad[:, CONV - 1 :]
    conv_grad = jnp.concatenate(
        [conv_part[:, : -(CONV - 1)], conv_part[:, -(CONV - 1) :] + edge_grad], axis=1
    )
    conv_low = conv_grad.astype(jnp.bfloat16)
    step_unactivated_gradient = step_raw_full.astype(jnp.bfloat16)
    inner_width = gate_preactivation.shape[-1]
    inner_convolved = conv_low[:, :, :inner_width]
    state_convolved = conv_low[:, :, inner_width:]
    gate_row_values = jnp.einsum(
        "yqr,yqj->rj",
        hidden_activation,
        gate_preactivation_gradient,
        preferred_element_type=jnp.float32,
    )
    inner_row_values = jnp.einsum(
        "yqr,yqj->rj", hidden_activation, inner_convolved, preferred_element_type=jnp.float32
    )
    entry_grad = jnp.stack([gate_row_values, inner_row_values], axis=1)
    state_weight_gradient = jnp.einsum(
        "yqr,yqj->rj", hidden_activation, state_convolved, preferred_element_type=jnp.float32
    )
    step_weight_gradient = jnp.einsum(
        "yfm,yfc->mc",
        hidden_activation,
        step_unactivated_gradient,
        preferred_element_type=jnp.float32,
    )
    hidden_part = jnp.einsum(
        "yjr,pr->yjp",
        gate_preactivation_gradient,
        entry_backward[:, 0],
        preferred_element_type=jnp.float32,
    )
    hidden_part = hidden_part + jnp.einsum(
        "yjr,pr->yjp", inner_convolved, entry_backward[:, 1], preferred_element_type=jnp.float32
    )
    hidden_part = hidden_part + jnp.einsum(
        "imr,vr->imv", step_unactivated_gradient, step_backward, preferred_element_type=jnp.float32
    )
    hidden_grad = lax.psum(hidden_part, "tensor")
    hidden_grad = hidden_grad + jnp.einsum(
        "yjr,pr->yjp", state_convolved, state_backward_weight, preferred_element_type=jnp.float32
    )
    norm_grad = jnp.sum(hidden_grad * inputs * scale, axis=(0, 1))
    normed_grad = hidden_grad * gain_back.astype(jnp.float32)
    token_grad = (
        cotangent.astype(jnp.float32)
        + scale * normed_grad
        - scale
        * scale
        * scale
        * inputs
        * jnp.sum(normed_grad * inputs, axis=-1, keepdims=True)
        / inputs.shape[-1]
    )
    shards = (
        lax.psum_scatter(norm_grad, ("dp", "context"), scatter_dimension=0, tiled=True),
        lax.psum_scatter(entry_grad, ("dp", "context"), scatter_dimension=0, tiled=True),
        lax.psum_scatter(state_weight_gradient, ("dp", "context"), scatter_dimension=0, tiled=True),
        lax.psum_scatter(step_weight_gradient, ("dp", "context"), scatter_dimension=0, tiled=True),
        lax.psum_scatter(exit_weight_gradient, ("dp", "context"), scatter_dimension=0, tiled=True),
    )
    smalls = lax.psum(
        (
            kernel_full[:, :inner_width],
            kernel_full[:, inner_width:],
            bias_grad,
            decay_grad,
            skip_grad,
            gate_grad,
        ),
        ("dp", "context"),
    )
    return (
        block_out,
        token_grad,
        shards[0],
        shards[1],
        shards[2],
        shards[3],
        smalls[0],
        smalls[1],
        smalls[2],
        smalls[3],
        smalls[4],
        smalls[5],
        shards[4],
    )


def solution(mesh):
    in_specs = (
        P("dp", "context", None),
        P("dp", "context"),
        P(("dp", "context")),
        P(("dp", "context"), None, "tensor"),
        P(("dp", "context"), None),
        P(("dp", "context"), "tensor"),
        P(None, "tensor"),
        P(),
        P("tensor"),
        P("tensor"),
        P("tensor"),
        P("tensor"),
        P(("dp", "context"), "tensor"),
        P("dp", "context", None),
    )
    out_specs = (
        P("dp", "context", None),
        P("dp", "context", None),
        P(("dp", "context")),
        P(("dp", "context"), None, "tensor"),
        P(("dp", "context"), None),
        P(("dp", "context"), "tensor"),
        P(None, "tensor"),
        P(),
        P("tensor"),
        P("tensor"),
        P("tensor"),
        P("tensor"),
        P(("dp", "context"), "tensor"),
    )
    return jax.shard_map(body, mesh=mesh, in_specs=in_specs, out_specs=out_specs, check_vma=False)
```

profile of v0, /device:TPU:0, one launch (start us, length us, event | category | flops | bytes accessed | tf_op | source)
XLA Modules:
  0.0 956.9 jit_solution(13679648080346581622)
XLA Ops:
  16.3 34.1 %all-reduce.37 = bf16[768]{0:T(1024)(128)(2,1)S(1)} all-reduce(bf16[768]{0:T(1024)(128)(2,1)S(1)} %dynamic-update-slice), channel_id=1, replica_groups=mesh['dp'=2,'context'=8,'tensor'=2] {'dp','context'}, use_global_device_ids=true, to_apply=%add.37 | all-reduce | flops 768 | bytes 3072
  51.2 17.4 %all-gather.2 = bf16[16,48,12]{1,2,0:T(8,128)(2,1)S(1)} all-gather(bf16[1,48,12]{1,2,0:T(8,128)(2,1)S(1)} %convert_bitcast_fusion), channel_id=1, replica_groups=mesh['dp'=2,'context'=8,'tensor'=2] {'dp','context'}, dimensions={0}, use_global_device_ids=true | all-gather | bytes 19584 | tf_op jit(solution)/shard_map/all_gather | solution.py:187
  78.7 20.7 %all_gather.40 = bf16[768,256]{1,0:T(8,128)(2,1)S(1)} all-gather(bf16[48,256]{1,0:T(8,128)(2,1)S(1)} %convert_element_type.95), channel_id=1, replica_groups=mesh['dp'=2,'context'=8,'tensor'=2] {'dp','context'}, dimensions={0}, use_global_device_ids=true | all-gather | bytes 417792 | tf_op jit(solution)/shard_map/all_gather | solution.py:186
  147.7 9.9 %all_gather.42 = f32[8,2,12]{2,1,0:T(2,128)} all-gather(f32[1,2,12]{2,1,0:T(2,128)S(1)} %fusion.186), channel_id=1, replica_groups=mesh['dp'=2,'context'=8,'tensor'=2] {'context'}, dimensions={0}, use_global_device_ids=true | all-gather | bytes 864 | tf_op jit(solution)/shard_map/all_gather | solution.py:22
  165.8 32.2 %all-gather.12.cloned.1.call-done = f32[16,12,64,128]{3,2,1,0:T(8,128)} async-done(((f32[2,12,64,128]{3,2,1,0:T(8,128)}), f32[16,12,64,128]{3,2,1,0:T(8,128)}) %all-gather.12.cloned.1.call-update) | async-done | bytes 6291472 | tf_op jit(solution)/shard_map/all_gather | solution.py:22
  198.0 14.4 %while.28 = (s32[]{:T(128)}, f32[2,12,64,128]{3,2,1,0:T(8,128)S(1)}, s32[]{:T(128)}, f32[8,2,12]{2,1,0:T(2,128)}, f32[8,2,12,64,128]{4,3,2,1,0:T(8,128)}, /*index=5*/s32[]{:T(128)}, s32[]{:T(128)}) while((s32[]{:T(128)}, f32[2,12,64,128]{3,2,1,0:T(8,128)S(1)}, s32[]{:T(128)}, f32[8,2,12]{2,1,0:T(2,128)}, ...), condition=%wide.region_6.7_spmd.clone, body=%wide.region_5.6_spmd.clone.sunk | while | flops 786436 | bytes 2359697 | solution.py:34
  214.9 9.6 %bitcast_add_fusion.3 = f32[2,256,12,64]{1,3,2,0:T(8,128)} fusion(f32[2,256,12,64]{1,3,2,0:T(8,128)S(1)} %fusion.151, f32[2,256,12,64]{1,3,2,0:T(8,128)S(1)} %bitcast.305, f32[2,12,256]{2,1,0:T(8,128)S(1)} %copy-done.82, f32[2,256,256]{2,1,0:T(8,128)} %fusion.169, f32[2,256,256]{2,1,0:T(8,128)S(1)} %copy-done.57, f32[2,12,256]{2,1,0:T(8,128)S(1)} %copy-done.84, ...), kind=kOutput, calls=%fused_computation.118 | convolution fusion | flops 1216610304 | bytes 5971968 | tf_op jit(solution)/shard_map/jvp(shtu,suhp->sthp)/dot_general | solution.py:85
  230.3 8.4 bitcast_add_fusion.2
  241.9 8.3 multiply_reduce_fusion.11
  255.3 6.6 multiply_reduce_fusion.8
  266.8 8.3 multiply_reduce_fusion.9
  292.9 12.6 %fusion.23 = (f32[2,12,256]{2,1,0:T(8,128)}, f32[2,12,256]{2,1,0:T(8,128)}, f32[2,12,256]{2,1,0:T(8,128)}, f32[2,256,256]{2,1,0:T(8,128)}) fusion(f32[2,12,256]{2,1,0:T(8,128)} %copy.340, f32[2,256,256]{2,1,0:T(8,128)} %fusion.169, f32[2,256,256]{2,1,0:T(8,128)} %get-tuple-element.429, f32[2,12,256]{2,1,0:T(8,128)} %copy.338, ...), kind=kOutput, calls=%fused_computation.50 | convolution fusion | flops 1231403008 | bytes 4972544 | tf_op jit(solution)/shard_map/transpose(jvp(shtu,suhp->sthp))/dot_general | solution.py:85
  310.3 8.3 fusion.13
  330.8 6.3 reduce-window.66
  345.1 13.2 %fusion.21 = (f32[2,12,256]{2,1,0:T(8,128)}, f32[2,12,256]{2,1,0:T(8,128)}, f32[2,12,256]{2,1,0:T(8,128)}, f32[2,256,256]{2,1,0:T(8,128)}) fusion(f32[2,12,256]{2,1,0:T(8,128)} %copy.355, f32[2,256,256]{2,1,0:T(8,128)} %fusion.159, f32[2,256,256]{2,1,0:T(8,128)} %get-tuple-element.432, f32[2,12,256]{2,1,0:T(8,128)} %copy.353, ...), kind=kOutput, calls=%fused_computation.48 | convolution fusion | flops 1231403008 | bytes 4972544 | tf_op jit(solution)/shard_map/transpose(jvp(shtu,suhp->sthp))/dot_general | solution.py:85
  365.4 6.3 reduce-window.60
  379.7 8.5 fusion.6
  418.6 6.6 rev.7
  425.1 14.0 %while.29 = (s32[]{:T(128)}, f32[2,12,64,128]{3,2,1,0:T(8,128)S(1)}, s32[]{:T(128)}, f32[8,2,12]{2,1,0:T(2,128)}, f32[8,2,12,64,128]{4,3,2,1,0:T(8,128)}, /*index=5*/s32[]{:T(128)}, s32[]{:T(128)}) while((s32[]{:T(128)}, f32[2,12,64,128]{3,2,1,0:T(8,128)S(1)}, s32[]{:T(128)}, f32[8,2,12]{2,1,0:T(2,128)}, ...), condition=%wide.region_16.17_spmd.clone, body=%wide.region_15.16_spmd.clone.sunk | while | flops 786436 | bytes 2359697 | solution.py:34
  458.0 5.6 multiply_reduce_fusion.14
  468.7 5.4 reduce-window.64
  508.4 5.7 multiply_add_fusion.1
  514.1 14.7 %all-reduce.47.cloned.1.call-done = (f32[2,512,128]{2,1,0:T(8,128)}, f32[2,512,128]{2,1,0:T(8,128)}) async-done(((f32[2,512,128]{2,1,0:T(8,128)}, f32[2,512,128]{2,1,0:T(8,128)}), (f32[2,512,128]{2,1,0:T(8,128)}, f32[2,512,128]{2,1,0:T(8,128)})) %all-reduce.47.cloned.1.call-update) | async-done | bytes 1048592 | tf_op jit(solution)/shard_map/psum | solution.py:274
  528.9 11.9 %multiply_reduce_fusion.7 = (f32[1024]{0:T(1024)S(1)}, f32[1024]{0:T(1024)S(1)}, f32[1024]{0:T(1024)S(1)}, f32[1024]{0:T(1024)S(1)}, f32[1024]{0:T(1024)S(1)}, /*index=5*/f32[2,512,1024]{2,1,0:T(8,128)S(1)}) fusion(f32[2,515,1024]{2,1,0:T(8,128)} %copy-done, f32[2,512]{1,0:T(2,128)S(1)} %get-tuple-element.440, f32[2,512]{1,0:T(2,128)S(1)} %get-tuple-element.441, ...), kind=kLoop, calls=%fused_computation.40 | loop fusion | flops 24112128 | bytes 29392896 | tf_op jit(solution)/shard_map/transpose(jvp())/reduce_sum | solution.py:43
  545.5 5.8 pad_add_fusion
  579.0 9.2 reduce-scatter.13.cloned.1.call-done
  593.1 150.2 %all-reduce.45.cloned.1.call-done = (f32[2,512,768]{2,1,0:T(8,128)}, f32[2,512,768]{2,1,0:T(8,128)}) async-done(((f32[2,512,768]{2,1,0:T(8,128)}, f32[2,512,768]{2,1,0:T(8,128)}), (f32[2,512,768]{2,1,0:T(8,128)}, f32[2,512,768]{2,1,0:T(8,128)})) %all-reduce.45.cloned.1.call-update) | async-done | bytes 6291472 | tf_op jit(solution)/shard_map/psum | solution.py:244
  743.4 5.9 fusion.32
  749.3 63.3 %all-reduce.39 = (f32[768]{0:T(1024)S(1)}, f32[5,768]{1,0:T(8,128)}, f32[5,256]{1,0:T(8,128)}, f32[12]{0:T(128)}, f32[12]{0:T(128)}, /*index=5*/f32[12]{0:T(128)}, f32[768]{0:T(1024)}) all-reduce(f32[768]{0:T(1024)S(1)} %get-tuple-element.400, ...), channel_id=4, replica_groups=mesh['dp'=2,'context'=8,'tensor'=2] {'dp','context'}, use_global_device_ids=true, to_apply=%region_45.46.clone | all-reduce | flops 6692 | bytes 53536
  813.2 7.0 fusion.30
  825.5 64.4 %reduce-scatter.15.cloned.1.call-done = f32[48,768]{1,0:T(8,128)} async-done(((f32[768,768]{1,0:T(8,128)}), f32[48,768]{1,0:T(8,128)}) %reduce-scatter.15.cloned.1.call-update) | async-done | bytes 147472
  889.9 60.0 %reduce-scatter.11.cloned.1.call-done = f32[48,256]{1,0:T(8,128)} async-done(((f32[768,256]{1,0:T(8,128)}), f32[48,256]{1,0:T(8,128)}) %reduce-scatter.11.cloned.1.call-update) | async-done | bytes 49168 | tf_op jit(solution)/shard_map/reduce_scatter | solution.py:344
  (488 shorter events, 312.6 us)
Async XLA Ops:
  7.2 66.3 %copy-start.112 = (f32[12]{0:T(128)S(1)}, f32[12]{0:T(128)}, u32[]{:S(2)}) copy-start(f32[12]{0:T(128)} %param.26) | copy-start | bytes 148
  7.2 100.6 %all-gather.8.cloned.1.call-start = ((), (), s32[]{:S(2)}) async-start(), calls=%async_computation.4 | async-start | bytes 2506752 | tf_op jit(solution)/shard_map/all_gather | solution.py:185
  8.0 93.2 %collective-permute-start.1 = (s32[2,3]{1,0:T(2,128)S(1)}, s32[2,3]{1,0:T(2,128)S(1)}, u32[]{:S(2)}, u32[]{:S(2)}) collective-permute-start(s32[2,3]{1,0:T(2,128)S(1)} %slice.211), channel_id=1, source_target_pairs={{0,2},{2,4},{4,6},{6,8},{8,10},{10,12},{12,14},{1,3},{3,5},{5,7},{... | collective-permute-start | bytes 80 | tf_op jit(solution)/shard_map/ppermute | solution.py:17
  12.0 186.0 %all-gather.12.cloned.1.call-start = ((), (), s32[]{:S(2)}) async-start(), calls=%async_computation.8 | async-start | bytes 7077888 | tf_op jit(solution)/shard_map/all_gather | solution.py:22
  13.4 61.3 %copy-start.114 = (f32[12]{0:T(128)}, f32[12]{0:T(128)S(1)}, u32[]{:S(2)}) copy-start(f32[12]{0:T(128)S(1)} %exp.91) | copy-start | bytes 148
  50.4 22.7 %copy-start.108 = (f32[768]{0:T(1024)}, f32[768]{0:T(1024)S(1)}, u32[]{:S(2)}) copy-start(f32[768]{0:T(1024)S(1)} %convert_element_type.92) | copy-start | bytes 9220
  74.8 33.0 %copy-start.20 = (f32[2,512,12]{2,0,1:T(2,128)}, f32[2,512,12]{2,0,1:T(2,128)S(1)}, u32[]{:S(2)}) copy-start(f32[2,512,12]{2,0,1:T(2,128)S(1)} %get-tuple-element.388) | copy-start | bytes 147460
  78.4 36.0 %copy-start.34 = (f32[2,12,256]{1,0,2:T(2,128)}, f32[2,12,256]{1,0,2:T(2,128)S(1)}, u32[]{:S(2)}) copy-start(f32[2,12,256]{1,0,2:T(2,128)S(1)} %copy.347) | copy-start | bytes 73732
  111.9 4.7 collective-permute-start
  135.6 23.7 %copy-start.50 = (f32[2,12,256]{1,0,2:T(2,128)S(1)}, f32[2,12,256]{1,0,2:T(2,128)}, u32[]{:S(2)}) copy-start(f32[2,12,256]{1,0,2:T(2,128)} %get-tuple-element.420) | copy-start | bytes 73732
  135.6 24.4 %copy-start.49 = (f32[2,256,12]{2,0,1:T(2,128)S(1)}, f32[2,256,12]{2,0,1:T(2,128)}, u32[]{:S(2)}) copy-start(f32[2,256,12]{2,0,1:T(2,128)} %get-tuple-element.426) | copy-start | bytes 73732
  135.6 24.5 %copy-start.48 = (f32[2,256,12]{2,0,1:T(2,128)S(1)}, f32[2,256,12]{2,0,1:T(2,128)}, u32[]{:S(2)}) copy-start(f32[2,256,12]{2,0,1:T(2,128)} %get-tuple-element.427) | copy-start | bytes 73732
  135.7 119.6 %all-gather.10.cloned.1.call-start = ((), (), s32[]{:S(2)}) async-start(), calls=%async_computation.5 | async-start | bytes 1253376 | tf_op jit(solution)/shard_map/all_gather | solution.py:188
  137.4 281.2 %all-gather.14.cloned.1.call-start = ((), (), s32[]{:S(2)}) async-start(), calls=%async_computation.9 | async-start | bytes 7077888 | tf_op jit(solution)/shard_map/all_gather | solution.py:22
  143.5 98.4 %copy-start.78 = (f32[768]{0:T(1024)}, f32[768]{0:T(1024)S(1)}, u32[]{:S(2)}) copy-start(f32[768]{0:T(1024)S(1)} %mul.876) | copy-start | bytes 9220
  160.2 54.7 %copy-start.60 = (f32[2,256,12]{1,2,0:T(8,128)}, f32[2,256,12]{1,2,0:T(8,128)S(1)}, u32[]{:S(2)}) copy-start(f32[2,256,12]{1,2,0:T(8,128)S(1)} %copy.343) | copy-start | bytes 73732
  198.0 16.9 %copy-start.57 = (f32[2,256,256]{2,1,0:T(8,128)S(1)}, f32[2,256,256]{2,1,0:T(8,128)}, u32[]{:S(2)}) copy-start(f32[2,256,256]{2,1,0:T(8,128)} %get-tuple-element.429) | copy-start | bytes 1572868
  198.0 16.9 %copy-start.65 = (pred[2,256,256]{2,1,0:T(8,128)(4,1)S(1)}, pred[2,256,256]{2,1,0:T(8,128)(4,1)}, u32[]{:S(2)}) copy-start(pred[2,256,256]{2,1,0:T(8,128)(4,1)} %get-tuple-element.428) | copy-start | bytes 393220
  198.0 16.9 %copy-start.82 = (f32[2,12,256]{2,1,0:T(8,128)S(1)}, f32[2,12,256]{2,1,0:T(8,128)}, u32[]{:S(2)}) copy-start(f32[2,12,256]{2,1,0:T(8,128)} %copy.340) | copy-start | bytes 73732
  198.0 16.9 %copy-start.84 = (f32[2,12,256]{2,1,0:T(8,128)S(1)}, f32[2,12,256]{2,1,0:T(8,128)}, u32[]{:S(2)}) copy-start(f32[2,12,256]{2,1,0:T(8,128)} %copy.338) | copy-start | bytes 73732
  241.9 13.4 %copy-start.96 = (f32[768]{0:T(1024)S(1)}, f32[768]{0:T(1024)}, u32[]{:S(2)}) copy-start(f32[768]{0:T(1024)} %param.29) | copy-start | bytes 9220
  291.3 237.6 %all-reduce.47.cloned.1.call-start = ((), (), s32[]{:S(2)}) async-start(), calls=%async_computation.13 | async-start | bytes 2097152 | tf_op jit(solution)/shard_map/psum | solution.py:274
  465.5 22.3 %copy-start.47 = (f32[2,256,128]{2,1,0:T(8,128)S(1)}, f32[2,256,128]{2,1,0:T(8,128)}, u32[]{:S(2)}) copy-start(f32[2,256,128]{2,1,0:T(8,128)} %fusion.103) | copy-start | bytes 786436
  489.8 98.4 %reduce-scatter.13.cloned.1.call-start = ((), (), s32[]{:S(2)}) async-start(), calls=%async_computation.10 | async-start | bytes 417792
  508.4 235.0 %all-reduce.45.cloned.1.call-start = ((), (), s32[]{:S(2)}) async-start(), calls=%async_computation.12 | async-start | bytes 12582912 | tf_op jit(solution)/shard_map/psum | solution.py:244
  544.2 9.4 collective-permute-start.2
  561.1 262.5 %reduce-scatter.9.cloned.1.call-start = ((), (), s32[]{:S(2)}) async-start(), calls=%async_computation.6 | async-start | bytes 5013504 | tf_op jit(solution)/shard_map/reduce_scatter | solution.py:343
  568.9 320.9 %reduce-scatter.15.cloned.1.call-start = ((), (), s32[]{:S(2)}) async-start(), calls=%async_computation.11 | async-start | bytes 2506752
  578.1 371.8 %reduce-scatter.11.cloned.1.call-start = ((), (), s32[]{:S(2)}) async-start(), calls=%async_computation.7 | async-start | bytes 835584 | tf_op jit(solution)/shard_map/reduce_scatter | solution.py:344
  589.8 153.6 %copy-start.31 = (bf16[2,512,768]{2,1,0:T(8,128)(2,1)S(1)}, bf16[2,512,768]{2,1,0:T(8,128)(2,1)}, u32[]{:S(2)}) copy-start(bf16[2,512,768]{2,1,0:T(8,128)(2,1)} %param.18) | copy-start | bytes 4718596
  589.8 153.6 %copy-start.43 = (bf16[768,256]{1,0:T(8,128)(2,1)S(1)}, bf16[768,256]{1,0:T(8,128)(2,1)}, u32[]{:S(2)}) copy-start(bf16[768,256]{1,0:T(8,128)(2,1)} %copy-done.42) | copy-start | bytes 1179652
  743.4 69.8 %copy-start.107 = (f32[2,512]{1,0:T(2,128)S(1)}, f32[2,512]{1,0:T(2,128)}, u32[]{:S(2)}) copy-start(f32[2,512]{1,0:T(2,128)} %get-tuple-element.444) | copy-start | bytes 12292
  (99 other events, 489.7 us)
Sparse Core Ops, SparseCore 0:
  12.1 45.0 all-gather.7
  135.8 62.1 all-gather.11
  200.3 37.0 all-gather.9
  291.4 63.4 all-gather.13
  490.0 38.8 all-reduce.46
  532.6 55.5 reduce-scatter.12
  590.7 152.5 all-reduce.44
  747.7 75.8 reduce-scatter.8
  827.9 61.9 reduce-scatter.14
  894.3 55.5 reduce-scatter.10
where the time goes:
time: 967 us; the launch traced here: 957 us
  waiting for transfers between devices  334 us (35%)
  matrix products  177 us (18%)
  blocking collectives  155 us (16%)
  other arithmetic  143 us (15%)
  local copies, waits for them, and re-layouts  122 us (13%)
  between operations  17.2 us (2%)
    psum x1, waiting for transfers between devices, body(): branch_path = lax.psum(partial_value_sum, 'tensor')  150 us
    unnamed x2, blocking collectives  97.4 us
    unnamed x12, waiting for transfers between devices  73.8 us
    dot_general x6, matrix products, span_output(): jnp.einsum('shtu,suhp->sthp', weights, values, precision=PRECISION_HIGH)  60.7 us
    reduce_scatter x1, waiting for transfers between devices, body(): lax.psum_scatter(state_weight_gradient, ('dp', 'context'), scatter_dimens...  60 us
    another operation x22, other arithmetic  36.2 us
    all_gather x2, waiting for transfers between devices, carried_in(): pieces = jax.tree.map(lambda part: lax.all_gather(part, axis), value)  32.2 us
    dot_general x8, matrix products, span_summary(): jnp.einsum('suh,suhp,sun->shpn', tail, values, writer, precision=PRECISIO...  29.6 us
  transfers between devices with their start and end apart: 13, of which 7 were waited for; matrix products, arithmetic and copies ran while one was open for 32% of the time, Pallas kernels for 0%

commit v1 on v0

--- a/solution.py
+++ b/solution.py
@@ -1,3 +1,4 @@
+import functools
 import jax
 import jax.numpy as jnp
 from jax import lax
@@ -9,6 +10,14 @@
 SPAN = 256
 EPSILON = 1e-05
 PRECISION_HIGH = lax.Precision.HIGHEST
+
+
+def return_all_patch(incoming_x, peer_axis):
+    odd = lax.all_gather(incoming_x, peer_axis)
+    return jnp.sum(odd, axis=0)
+
+
+keep_up_space = functools.partial(return_all_patch, peer_axis="tensor")
 
 
 def passed_along(x, axis, by):
@@ -241,7 +250,7 @@
     partial_value_sum = jnp.einsum(
         "yjr,pr->yjp", unit_activation, exit_reduced, preferred_element_type=jnp.float32
     )
-    branch_path = lax.psum(partial_value_sum, "tensor")
+    branch_path = keep_up_space(partial_value_sum)
     block_out = (inputs + branch_path).astype(jnp.bfloat16)
     gain_back, entry_backward, state_backward_weight, step_backward, exit_backward = (
         lax.all_gather(masters[0], ("dp", "context"), axis=0, tiled=True),

time: 967 us -> 879 us (0.909)
  waiting for transfers between devices: 334 us -> 238 us
    psum x1, waiting for transfers between devices: 150 us -> 71.4 us  [body(): hidden_grad = lax.psum(hidden_part, 'tensor')]
    psum x1, waiting for transfers between devices: 14.7 us -> 0.01 us  [body(): lax.psum((writer_one + writer_two, reader_one), 'tensor')]
    unnamed x12 -> x13, waiting for transfers between devices: 73.8 us -> 64.4 us
    unnamed x244 -> x270, local copies, waits for them, and re-layouts: 20.9 us -> 21.8 us
  transfers between devices with their start and end apart: 13 -> 14, of which waited for: 7 -> 6; matrix products, arithmetic and copies ran while one was open for 32% -> 41% of each run, Pallas kernels for 0% -> 0%
where the time goes in v1:
time: 879 us; the launch traced here: 869 us
  waiting for transfers between devices  238 us (27%)
  matrix products  178 us (20%)
  blocking collectives  156 us (18%)
  other arithmetic  149 us (17%)
  local copies, waits for them, and re-layouts  122 us (14%)
  between operations  17.1 us (2%)
    unnamed x2, blocking collectives  97.8 us
    psum x1, waiting for transfers between devices, body(): hidden_grad = lax.psum(hidden_part, 'tensor')  71.4 us
    unnamed x13, waiting for transfers between devices  64.4 us
    reduce_scatter x1, waiting for transfers between devices, body(): lax.psum_scatter(state_weight_gradient, ('dp', 'context'), scatter_dimens...  60.1 us
    dot_general x6, matrix products, span_output(): jnp.einsum('shtu,suhp->sthp', weights, values, precision=PRECISION_HIGH)  58.7 us
    all_gather x2, waiting for transfers between devices, carried_in(): pieces = jax.tree.map(lambda part: lax.all_gather(part, axis), value)  39.8 us
    another operation x22, other arithmetic  35.2 us
    dot_general x8, matrix products, span_summary(): jnp.einsum('suh,suhp,sun->shpn', tail, values, writer, precision=PRECISIO...  28.1 us
  transfers between devices with their start and end apart: 14, of which 6 were waited for; matrix products, arithmetic and copies ran while one was open for 41% of the time, Pallas kernels for 0%

profile of v1, /device:TPU:0, one launch (start us, length us, event | category | flops | bytes accessed | tf_op | source)
XLA Modules:
  0.0 868.9 jit_solution(17238468746078848659)
XLA Ops:
  16.3 34.1 %all-reduce.37 = bf16[768]{0:T(1024)(128)(2,1)S(1)} all-reduce(bf16[768]{0:T(1024)(128)(2,1)S(1)} %dynamic-update-slice), channel_id=1, replica_groups=mesh['dp'=2,'context'=8,'tensor'=2] {'dp','context'}, use_global_device_ids=true, to_apply=%add.37 | all-reduce | flops 768 | bytes 3072
  51.2 17.4 %all-gather.3 = bf16[16,48,12]{1,2,0:T(8,128)(2,1)S(1)} all-gather(bf16[1,48,12]{1,2,0:T(8,128)(2,1)S(1)} %convert_bitcast_fusion), channel_id=1, replica_groups=mesh['dp'=2,'context'=8,'tensor'=2] {'dp','context'}, dimensions={0}, use_global_device_ids=true | all-gather | bytes 19584 | tf_op jit(solution)/shard_map/all_gather | solution.py:196
  78.7 20.7 %all_gather.46 = bf16[768,256]{1,0:T(8,128)(2,1)S(1)} all-gather(bf16[48,256]{1,0:T(8,128)(2,1)S(1)} %convert_element_type.95), channel_id=1, replica_groups=mesh['dp'=2,'context'=8,'tensor'=2] {'dp','context'}, dimensions={0}, use_global_device_ids=true | all-gather | bytes 417792 | tf_op jit(solution)/shard_map/all_gather | solution.py:195
  147.7 9.9 %all_gather.48 = f32[8,2,12]{2,1,0:T(2,128)} all-gather(f32[1,2,12]{2,1,0:T(2,128)S(1)} %fusion.186), channel_id=1, replica_groups=mesh['dp'=2,'context'=8,'tensor'=2] {'context'}, dimensions={0}, use_global_device_ids=true | all-gather | bytes 864 | tf_op jit(solution)/shard_map/all_gather | solution.py:31
  165.7 32.1 %all-gather.14.cloned.1.call-done = f32[16,12,64,128]{3,2,1,0:T(8,128)} async-done(((f32[2,12,64,128]{3,2,1,0:T(8,128)}), f32[16,12,64,128]{3,2,1,0:T(8,128)}) %all-gather.14.cloned.1.call-update) | async-done | bytes 6291472 | tf_op jit(solution)/shard_map/all_gather | solution.py:31
  197.9 14.4 %while.28 = (s32[]{:T(128)}, f32[2,12,64,128]{3,2,1,0:T(8,128)S(1)}, s32[]{:T(128)}, f32[8,2,12]{2,1,0:T(2,128)}, f32[8,2,12,64,128]{4,3,2,1,0:T(8,128)}, /*index=5*/s32[]{:T(128)}, s32[]{:T(128)}) while((s32[]{:T(128)}, f32[2,12,64,128]{3,2,1,0:T(8,128)S(1)}, s32[]{:T(128)}, f32[8,2,12]{2,1,0:T(2,128)}, ...), condition=%wide.region_6.7_spmd.clone, body=%wide.region_5.6_spmd.clone.sunk | while | flops 786436 | bytes 2359697 | solution.py:43
  214.7 9.6 %bitcast_add_fusion.3 = f32[2,256,12,64]{1,3,2,0:T(8,128)} fusion(f32[2,256,12,64]{1,3,2,0:T(8,128)S(1)} %fusion.151, f32[2,256,12,64]{1,3,2,0:T(8,128)S(1)} %bitcast.306, f32[2,12,256]{2,1,0:T(8,128)S(1)} %copy-done.97, f32[2,256,256]{2,1,0:T(8,128)} %fusion.169, f32[2,256,256]{2,1,0:T(8,128)S(1)} %copy-done.62, f32[2,12,256]{2,1,0:T(8,128)S(1)} %copy-done.100, ...), kind=kOutput, calls=%fused_computation.118 | convolution fusion | flops 1216610304 | bytes 5971968 | tf_op jit(solution)/shard_map/jvp(shtu,suhp->sthp)/dot_general | solution.py:94
  230.2 8.4 bitcast_add_fusion.2
  241.7 8.3 multiply_reduce_fusion.11
  255.2 6.6 multiply_reduce_fusion.8
  266.7 8.3 multiply_reduce_fusion.9
  292.6 12.6 %fusion.23 = (f32[2,12,256]{2,1,0:T(8,128)}, f32[2,12,256]{2,1,0:T(8,128)}, f32[2,12,256]{2,1,0:T(8,128)}, f32[2,256,256]{2,1,0:T(8,128)}) fusion(f32[2,12,256]{2,1,0:T(8,128)} %copy.340, f32[2,256,256]{2,1,0:T(8,128)} %fusion.169, f32[2,256,256]{2,1,0:T(8,128)} %get-tuple-element.427, f32[2,12,256]{2,1,0:T(8,128)} %copy.338, ...), kind=kOutput, calls=%fused_computation.50 | convolution fusion | flops 1231403008 | bytes 4972544 | tf_op jit(solution)/shard_map/transpose(jvp(shtu,suhp->sthp))/dot_general | solution.py:94
  324.1 11.6 %fusion.21 = (f32[2,12,256]{2,1,0:T(8,128)}, f32[2,12,256]{2,1,0:T(8,128)}, f32[2,12,256]{2,1,0:T(8,128)}, f32[2,256,256]{2,1,0:T(8,128)S(1)}) fusion(f32[2,12,256]{2,1,0:T(8,128)S(1)} %copy-done.96, f32[2,256,256]{2,1,0:T(8,128)S(1)} %copy-done.61, f32[2,256,256]{2,1,0:T(8,128)S(1)} %copy-done.59, f32[2,12,256]{2,1,0:T(8,128)S(1)} %copy-done.99, ...), kind=kOutput, calls=%fused_computation.48 | convolution fusion | flops 1231403008 | bytes 4972544 | tf_op jit(solution)/shard_map/transpose(jvp(shtu,suhp->sthp))/dot_general | solution.py:94
  346.9 7.7 all-gather.18.cloned.1.call-done
  354.6 6.6 rev.7
  361.1 14.2 %while.29 = (s32[]{:T(128)}, f32[2,12,64,128]{3,2,1,0:T(8,128)S(1)}, s32[]{:T(128)}, f32[8,2,12]{2,1,0:T(2,128)}, f32[8,2,12,64,128]{4,3,2,1,0:T(8,128)}, /*index=5*/s32[]{:T(128)}, s32[]{:T(128)}) while((s32[]{:T(128)}, f32[2,12,64,128]{3,2,1,0:T(8,128)S(1)}, s32[]{:T(128)}, f32[8,2,12]{2,1,0:T(2,128)}, ...), condition=%wide.region_16.17_spmd.clone, body=%wide.region_15.16_spmd.clone.sunk | while | flops 786436 | bytes 2359697 | solution.py:43
  387.2 6.3 reduce-window.66
  393.5 5.4 fusion.98
  398.9 8.3 fusion.13
  425.8 6.4 reduce-window.60
  439.1 8.2 fusion.6
  514.0 5.7 multiply_add_fusion.1
  519.7 11.9 %multiply_reduce_fusion.7 = (f32[1024]{0:T(1024)S(1)}, f32[1024]{0:T(1024)S(1)}, f32[1024]{0:T(1024)S(1)}, f32[1024]{0:T(1024)S(1)}, f32[1024]{0:T(1024)S(1)}, /*index=5*/f32[2,512,1024]{2,1,0:T(8,128)S(1)}) fusion(f32[2,515,1024]{2,1,0:T(8,128)} %copy-done, f32[2,512]{1,0:T(2,128)S(1)} %get-tuple-element.438, f32[2,512]{1,0:T(2,128)S(1)} %get-tuple-element.439, ...), kind=kLoop, calls=%fused_computation.40 | loop fusion | flops 24112128 | bytes 29392896 | tf_op jit(solution)/shard_map/transpose(jvp())/reduce_sum | solution.py:52
  536.4 5.8 pad_add_fusion
  560.6 5.4 convolution_bitcast_fusion
  570.5 5.5 reduce_sum.296
  584.1 71.4 %all-reduce.44.cloned.1.call-done = f32[2,512,768]{2,1,0:T(8,128)} async-done(((f32[2,512,768]{2,1,0:T(8,128)}), f32[2,512,768]{2,1,0:T(8,128)}) %all-reduce.44.cloned.1.call-update) | async-done | bytes 3145744 | tf_op jit(solution)/shard_map/psum | solution.py:334
  655.5 5.6 fusion.32
  661.1 63.7 %all-reduce.39 = (f32[768]{0:T(1024)S(1)}, f32[5,768]{1,0:T(8,128)}, f32[5,256]{1,0:T(8,128)}, f32[12]{0:T(128)}, f32[12]{0:T(128)}, /*index=5*/f32[12]{0:T(128)}, f32[768]{0:T(1024)}) all-reduce(f32[768]{0:T(1024)S(1)} %get-tuple-element.398, ...), channel_id=5, replica_groups=mesh['dp'=2,'context'=8,'tensor'=2] {'dp','context'}, use_global_device_ids=true, to_apply=%region_45.46.clone | all-reduce | flops 6692 | bytes 53536
  725.3 7.9 fusion.30
  737.7 64.2 %reduce-scatter.15.cloned.1.call-done = f32[48,768]{1,0:T(8,128)} async-done(((f32[768,768]{1,0:T(8,128)}), f32[48,768]{1,0:T(8,128)}) %reduce-scatter.15.cloned.1.call-update) | async-done | bytes 147472
  802.0 60.1 %reduce-scatter.11.cloned.1.call-done = f32[48,256]{1,0:T(8,128)} async-done(((f32[768,256]{1,0:T(8,128)}), f32[48,256]{1,0:T(8,128)}) %reduce-scatter.11.cloned.1.call-update) | async-done | bytes 49168 | tf_op jit(solution)/shard_map/reduce_scatter | solution.py:353
  (517 shorter events, 315.1 us)
Async XLA Ops:
  7.2 66.3 %copy-start.125 = (f32[12]{0:T(128)S(1)}, f32[12]{0:T(128)}, u32[]{:S(2)}) copy-start(f32[12]{0:T(128)} %param.26) | copy-start | bytes 148
  7.2 100.5 %all-gather.10.cloned.1.call-start = ((), (), s32[]{:S(2)}) async-start(), calls=%async_computation.4 | async-start | bytes 2506752 | tf_op jit(solution)/shard_map/all_gather | solution.py:194
  8.0 93.1 %collective-permute-start.1 = (s32[2,3]{1,0:T(2,128)S(1)}, s32[2,3]{1,0:T(2,128)S(1)}, u32[]{:S(2)}, u32[]{:S(2)}) collective-permute-start(s32[2,3]{1,0:T(2,128)S(1)} %slice.211), channel_id=1, source_target_pairs={{0,2},{2,4},{4,6},{6,8},{8,10},{10,12},{12,14},{1,3},{3,5},{5,7},{... | collective-permute-start | bytes 80 | tf_op jit(solution)/shard_map/ppermute | solution.py:26
  12.0 185.9 %all-gather.14.cloned.1.call-start = ((), (), s32[]{:S(2)}) async-start(), calls=%async_computation.9 | async-start | bytes 7077888 | tf_op jit(solution)/shard_map/all_gather | solution.py:31
  13.4 61.3 %copy-start.127 = (f32[12]{0:T(128)}, f32[12]{0:T(128)S(1)}, u32[]{:S(2)}) copy-start(f32[12]{0:T(128)S(1)} %exp.91) | copy-start | bytes 148
  74.8 32.9 %copy-start.21 = (f32[2,512,12]{2,0,1:T(2,128)}, f32[2,512,12]{2,0,1:T(2,128)S(1)}, u32[]{:S(2)}) copy-start(f32[2,512,12]{2,0,1:T(2,128)S(1)} %get-tuple-element.386) | copy-start | bytes 147460
  78.4 35.9 %copy-start.33 = (f32[2,12,256]{1,0,2:T(2,128)}, f32[2,12,256]{1,0,2:T(2,128)S(1)}, u32[]{:S(2)}) copy-start(f32[2,12,256]{1,0,2:T(2,128)S(1)} %copy.347) | copy-start | bytes 73732
  111.7 4.7 collective-permute-start
  135.6 23.7 %copy-start.54 = (f32[2,12,256]{1,0,2:T(2,128)S(1)}, f32[2,12,256]{1,0,2:T(2,128)}, u32[]{:S(2)}) copy-start(f32[2,12,256]{1,0,2:T(2,128)} %get-tuple-element.418) | copy-start | bytes 73732
  135.6 24.4 %copy-start.53 = (f32[2,256,12]{2,0,1:T(2,128)S(1)}, f32[2,256,12]{2,0,1:T(2,128)}, u32[]{:S(2)}) copy-start(f32[2,256,12]{2,0,1:T(2,128)} %get-tuple-element.424) | copy-start | bytes 73732
  135.6 24.5 %copy-start.52 = (f32[2,256,12]{2,0,1:T(2,128)S(1)}, f32[2,256,12]{2,0,1:T(2,128)}, u32[]{:S(2)}) copy-start(f32[2,256,12]{2,0,1:T(2,128)} %get-tuple-element.425) | copy-start | bytes 73732
  135.6 119.5 %all-gather.12.cloned.1.call-start = ((), (), s32[]{:S(2)}) async-start(), calls=%async_computation.5 | async-start | bytes 1253376 | tf_op jit(solution)/shard_map/all_gather | solution.py:197
  137.3 217.3 %all-gather.18.cloned.1.call-start = ((), (), s32[]{:S(2)}) async-start(), calls=%async_computation.11 | async-start | bytes 7077888 | tf_op jit(solution)/shard_map/all_gather | solution.py:31
  143.4 98.3 %copy-start.92 = (f32[768]{0:T(1024)}, f32[768]{0:T(1024)S(1)}, u32[]{:S(2)}) copy-start(f32[768]{0:T(1024)S(1)} %mul.876) | copy-start | bytes 9220
  160.1 54.6 %copy-start.63 = (f32[2,256,12]{1,2,0:T(8,128)}, f32[2,256,12]{1,2,0:T(8,128)S(1)}, u32[]{:S(2)}) copy-start(f32[2,256,12]{1,2,0:T(8,128)S(1)} %copy.343) | copy-start | bytes 73732
  255.1 138.4 %copy-start.90 = (f32[2,512]{1,0:T(2,128)}, f32[2,512]{1,0:T(2,128)S(1)}, u32[]{:S(2)}) copy-start(f32[2,512]{1,0:T(2,128)S(1)} %get-tuple-element.445) | copy-start | bytes 12292
  291.0 228.7 %all-reduce.46.cloned.1.call-start = ((), (), s32[]{:S(2)}) async-start(), calls=%async_computation.14 | async-start | bytes 2097152 | tf_op jit(solution)/shard_map/psum | solution.py:283
  383.4 187.0 %all-gather.16.cloned.1.call-start = ((), (), s32[]{:S(2)}) async-start(), calls=%async_computation.10 | async-start | bytes 9437184 | tf_op jit(solution)/shard_map/all_gather | solution.py:16
  407.3 169.2 %reduce-scatter.13.cloned.1.call-start = ((), (), s32[]{:S(2)}) async-start(), calls=%async_computation.12 | async-start | bytes 417792
  513.9 141.6 %all-reduce.44.cloned.1.call-start = ((), (), s32[]{:S(2)}) async-start(), calls=%async_computation.6 | async-start | bytes 6291456 | tf_op jit(solution)/shard_map/psum | solution.py:334
  531.6 46.3 %copy-start.83 = (f32[1024]{0:T(1024)}, f32[1024]{0:T(1024)S(1)}, u32[]{:S(2)}) copy-start(f32[1024]{0:T(1024)S(1)} %get-tuple-element.318) | copy-start | bytes 12292
  531.7 46.3 %copy-start.85 = (f32[1024]{0:T(1024)}, f32[1024]{0:T(1024)S(1)}, u32[]{:S(2)}) copy-start(f32[1024]{0:T(1024)S(1)} %get-tuple-element.319) | copy-start | bytes 12292
  531.7 46.3 %copy-start.87 = (f32[1024]{0:T(1024)}, f32[1024]{0:T(1024)S(1)}, u32[]{:S(2)}) copy-start(f32[1024]{0:T(1024)S(1)} %get-tuple-element.320) | copy-start | bytes 12292
  531.7 46.3 %copy-start.89 = (f32[1024]{0:T(1024)}, f32[1024]{0:T(1024)S(1)}, u32[]{:S(2)}) copy-start(f32[1024]{0:T(1024)S(1)} %get-tuple-element.331) | copy-start | bytes 12292
  535.2 9.4 %collective-permute-start.2 = (f32[2,3,1024]{2,1,0:T(4,128)S(1)}, f32[2,3,1024]{2,1,0:T(4,128)S(1)}, u32[]{:S(2)}, u32[]{:S(2)}) collective-permute-start(f32[2,3,1024]{2,1,0:T(4,128)S(1)} %pad_add_fusion.5), channel_id=1, source_target_pairs={{2,0},{4,2},{6,4},{8,6},{10,8},{12,10},{14,12},{3,1},{5,3},{7,5},{... | collective-permute-start | bytes 73736 | tf_op jit(solution)/shard_map/ppermute | solution.py:26
  552.0 183.8 %reduce-scatter.9.cloned.1.call-start = ((), (), s32[]{:S(2)}) async-start(), calls=%async_computation.7 | async-start | bytes 5013504 | tf_op jit(solution)/shard_map/reduce_scatter | solution.py:352
  559.9 242.1 %reduce-scatter.15.cloned.1.call-start = ((), (), s32[]{:S(2)}) async-start(), calls=%async_computation.13 | async-start | bytes 2506752
  569.0 293.0 %reduce-scatter.11.cloned.1.call-start = ((), (), s32[]{:S(2)}) async-start(), calls=%async_computation.8 | async-start | bytes 835584 | tf_op jit(solution)/shard_map/reduce_scatter | solution.py:353
  579.5 76.0 %copy-start.24 = (f32[2,512,768]{2,1,0:T(8,128)S(1)}, f32[2,512,768]{2,1,0:T(8,128)}, u32[]{:S(2)}) copy-start(f32[2,512,768]{2,1,0:T(8,128)} %reduce_sum.296) | copy-start | bytes 9437188
  579.5 76.0 %copy-start.41 = (bf16[768,256]{1,0:T(8,128)(2,1)S(1)}, bf16[768,256]{1,0:T(8,128)(2,1)}, u32[]{:S(2)}) copy-start(bf16[768,256]{1,0:T(8,128)(2,1)} %copy-done.40) | copy-start | bytes 1179652
  584.1 77.0 %copy-start.101 = (f32[5,256]{1,0:T(8,128)S(1)}, f32[5,256]{1,0:T(8,128)}, u32[]{:S(2)}) copy-start(f32[5,256]{1,0:T(8,128)} %pad_add_fusion.7) | copy-start | bytes 15364
  584.1 141.2 %copy-start.112 = (f32[2,512]{1,0:T(2,128)S(1)}, f32[2,512]{1,0:T(2,128)}, u32[]{:S(2)}) copy-start(f32[2,512]{1,0:T(2,128)} %copy-done.109) | copy-start | bytes 12292
  (112 other events, 743.8 us)
Sparse Core Ops, SparseCore 0:
  12.1 45.0 all-gather.9
  135.8 62.0 all-gather.13
  200.2 37.0 all-gather.11
  291.1 63.4 all-gather.17
  383.5 38.8 all-reduce.45
  423.9 80.3 all-gather.15
  514.0 54.2 reduce-scatter.12
  570.6 84.7 all-reduce.43
  659.8 75.9 reduce-scatter.8
  740.0 61.9 reduce-scatter.14
  806.5 55.5 reduce-scatter.10
